TPU v7x, 32 devices: a whole 2x2x4 slice. The times are simulated.
32 devices in a mesh: dp: 16 (over z, y, x), tensor: 2 (over core).
Axes of the slice: x: 2, y: 2, z: 4, core: 2. Of those that a mesh axis runs over, the one named last changes fastest.
Arguments:
- inputs: bfloat16 [17664, 1024], P(('dp', 'tensor')), may hold values from -6 to 6
- cotangent: bfloat16 [17664, 1024], P(('dp', 'tensor')), may hold values from -6 to 6
- slot_live: int32 [16], P('dp'), may hold values from 0 to 1, as said below
- token_type: int32 [17664], P(('dp', 'tensor')), may hold values from 0 to 3, as said below
- attn_norm_gain: bfloat16 [1024], P('dp'), may hold values from 0.25 to 1.75
- attn_norm_bias: bfloat16 [1024], P('dp'), may hold values from -4 to 4
- qkv_weight: bfloat16 [3, 1024, 1024], P(None, 'dp', 'tensor'), may hold values from -0.1875 to 0.1875
- proj_weight: bfloat16 [1024, 1024], P('tensor', 'dp'), may hold values from -1 to 1
- proj_bias: bfloat16 [1024], P('dp'), may hold values from -4 to 4
- mlp_norm_gain: bfloat16 [1024], P('dp'), may hold values from 0.25 to 1.75
- mlp_norm_bias: bfloat16 [1024], P('dp'), may hold values from -4 to 4
- fc1_weight: bfloat16 [1024, 4096], P('dp', 'tensor'), may hold values from -0.1875 to 0.1875
- fc1_bias: bfloat16 [4096], P(('tensor', 'dp')), may hold values from -6 to 6
- fc2_weight: bfloat16 [4096, 1024], P('tensor', 'dp'), may hold values from -0.09375 to 0.09375
- fc2_bias: bfloat16 [1024], P('dp'), may hold values from -4 to 4
Outputs:
- outputs: bfloat16 [17664, 1024], P(('dp', 'tensor'))
- grad_inputs: bfloat16 [17664, 1024], P(('dp', 'tensor'))
- grad_attn_norm_gain: float32 [1024], P('dp')
- grad_attn_norm_bias: float32 [1024], P('dp')
- grad_qkv_weight: float32 [3, 1024, 1024], P(None, 'dp', 'tensor')
- grad_proj_weight: float32 [1024, 1024], P('tensor', 'dp')
- grad_proj_bias: float32 [1024], P('dp')
- grad_mlp_norm_gain: float32 [1024], P('dp')
- grad_mlp_norm_bias: float32 [1024], P('dp')
- grad_fc1_weight: float32 [1024, 4096], P('dp', 'tensor')
- grad_fc1_bias: float32 [4096], P(('tensor', 'dp'))
- grad_fc2_weight: float32 [4096, 1024], P('tensor', 'dp')
- grad_fc2_bias: float32 [1024], P('dp')
Inputs may be any that keep to these rules, and one draw needn't show every extreme that they name: `slot_live`: the ones of each data group's 1 entries come first; some data group holds 1 sequence. `token_type`: in each sequence position 0 is 0; positions 1 to 77 are 1 up to a caption length of at least one and 3 after it; later positions are 2, except the last two, which are 3.
All inputs are finite; a program needn't handle non-finite values.
Results may differ from a plain program's by a relative error of at most 0.02.
Values may be sent and summed in bfloat16 or wider, within the bound.
No kernel may reach another device: no remote copies, remote signals or barrier semaphores. Data moves between devices by JAX's collectives and lax.ppermute only.
A program may use at most 256 MiB of HBM per device.

v0:
```python
import jax
import jax.numpy as jnp
from jax import lax
from jax.sharding import PartitionSpec as P

HEAD_DIM = 64
SEQ_LEN = 1104


def layer_norm(values, norm_gain, norm_shift):
    row_mean = jnp.mean(values, axis=-1, keepdims=True)
    centered = values - row_mean
    variance = jnp.mean(centered * centered, axis=-1, keepdims=True)
    return centered * lax.rsqrt(variance + 1e-05) * norm_gain + norm_shift


def exact_gelu(values):
    return jax.nn.gelu(values, approximate=False)


def masked_scores(query, keys, key_valid, score_scale):
    scores = (
        jnp.einsum("qhd,khd->hqk", query, keys, preferred_element_type=jnp.float32) * score_scale
    )
    return jnp.where(key_valid[None, None, :] > 0, scores, -1e30)


def attend_forward(query, keys, values, key_valid, score_scale):
    scores = masked_scores(query, keys, key_valid, score_scale)
    row_max = jnp.max(scores, axis=-1, keepdims=True)
    exp_scores = jnp.exp(scores - row_max)
    row_sum = jnp.sum(exp_scores, axis=-1, keepdims=True)
    attn_prob = (exp_scores / row_sum).astype(jnp.bfloat16)
    mixed = jnp.einsum("hqk,khd->qhd", attn_prob, values, preferred_element_type=jnp.float32)
    return (mixed.astype(jnp.bfloat16), row_max + jnp.log(row_sum))


def attend_backward(query, keys, values, key_valid, log_total, grad_mixed, score_scale):
    scores = masked_scores(query, keys, key_valid, score_scale)
    attn_prob = jnp.exp(scores - log_total)
    grad_prob = jnp.einsum("qhd,khd->hqk", grad_mixed, values, preferred_element_type=jnp.float32)
    row_dot = jnp.sum(attn_prob * grad_prob, axis=-1, keepdims=True)
    grad_scores = (attn_prob * (grad_prob - row_dot)).astype(jnp.bfloat16)
    grad_query = (
        jnp.einsum("hqk,khd->qhd", grad_scores, keys, preferred_element_type=jnp.float32)
        * score_scale
    )
    grad_keys = (
        jnp.einsum("hqk,qhd->khd", grad_scores, query, preferred_element_type=jnp.float32)
        * score_scale
    )
    grad_values = jnp.einsum(
        "hqk,qhd->khd",
        attn_prob.astype(jnp.bfloat16),
        grad_mixed,
        preferred_element_type=jnp.float32,
    )
    return (
        grad_query.astype(jnp.bfloat16),
        grad_keys.astype(jnp.bfloat16),
        grad_values.astype(jnp.bfloat16),
    )


def contract_rows(left, right):
    return lax.dot_general(
        left, right, (((0,), (0,)), ((), ())), preferred_element_type=jnp.float32
    )


def contract_cols(left, right):
    return lax.dot_general(
        left, right, (((1,), (1,)), ((), ())), preferred_element_type=jnp.float32
    )


def on_device(
    inputs,
    cotangent,
    slot_live,
    token_type,
    attn_norm_gain,
    attn_norm_bias,
    qkv_weight,
    proj_weight,
    proj_bias,
    mlp_norm_gain,
    mlp_norm_bias,
    fc1_weight,
    fc1_bias,
    fc2_weight,
    fc2_bias,
):
    tensor_size = lax.axis_size("tensor")
    tensor_rank = lax.axis_index("tensor")
    local_rows = inputs.shape[0]
    slot_count = slot_live.shape[0]
    whole_rows = local_rows * tensor_size
    width_here = qkv_weight.shape[2]
    heads_here = width_here // HEAD_DIM
    score_scale = HEAD_DIM ** (-0.5)
    position = tensor_rank * local_rows + jnp.arange(local_rows, dtype=jnp.int32)
    slot_of_row = position // SEQ_LEN
    slot_match = slot_of_row[:, None] == jnp.arange(slot_count, dtype=jnp.int32)[None, :]
    live_rows = jnp.sum(jnp.where(slot_match, slot_live.astype(jnp.float32)[None, :], 0.0), axis=1)
    live_col = live_rows[:, None]
    valid_local = (token_type != 3).astype(jnp.bfloat16)
    (
        qkv_full,
        proj_full,
        proj_bias_full,
        gain_one,
        shift_one,
        fc1_full,
        fc1_bias_full,
        fc2_full,
        gain_two,
        shift_two,
        fc2_bias_full,
    ) = (
        lax.all_gather(qkv_weight, "dp", axis=1, tiled=True),
        lax.all_gather(proj_weight, "dp", axis=1, tiled=True),
        lax.all_gather(proj_bias, "dp", axis=0, tiled=True),
        lax.all_gather(attn_norm_gain, "dp", axis=0, tiled=True),
        lax.all_gather(attn_norm_bias, "dp", axis=0, tiled=True),
        lax.all_gather(fc1_weight, "dp", axis=0, tiled=True),
        lax.all_gather(fc1_bias, "dp", axis=0, tiled=True),
        lax.all_gather(fc2_weight, "dp", axis=1, tiled=True),
        lax.all_gather(mlp_norm_gain, "dp", axis=0, tiled=True),
        lax.all_gather(mlp_norm_bias, "dp", axis=0, tiled=True),
        lax.all_gather(fc2_bias, "dp", axis=0, tiled=True),
    )
    gain_one_f = gain_one.astype(jnp.float32)
    shift_one_f = shift_one.astype(jnp.float32)
    rows_in = inputs.astype(jnp.float32)
    norm_one = layer_norm(rows_in, gain_one_f, shift_one_f).astype(jnp.bfloat16)
    whole_one, whole_valid = (
        lax.all_gather(norm_one, "tensor", axis=0, tiled=True),
        lax.all_gather(valid_local, "tensor", axis=0, tiled=True),
    )
    packed = jnp.einsum("nd,jdc->jnc", whole_one, qkv_full, preferred_element_type=jnp.float32)
    packed = packed.astype(jnp.bfloat16).reshape(3, slot_count, SEQ_LEN, heads_here, HEAD_DIM)
    valid_seq = whole_valid.reshape(slot_count, SEQ_LEN)

    def forward_slot(slot_index):
        slot_qkv = lax.dynamic_index_in_dim(packed, slot_index, 1, keepdims=False)
        slot_valid = lax.dynamic_index_in_dim(valid_seq, slot_index, 0, keepdims=False)
        return attend_forward(slot_qkv[0], slot_qkv[1], slot_qkv[2], slot_valid, score_scale)

    heads_out, log_total = lax.map(forward_slot, jnp.arange(slot_count, dtype=jnp.int32))
    mixed_flat = heads_out.reshape(whole_rows, width_here)
    row_block = mixed_flat
    attn_out = lax.psum_scatter(
        jnp.dot(row_block, proj_full, preferred_element_type=jnp.float32).astype(jnp.bfloat16),
        "tensor",
        scatter_dimension=0,
        tiled=True,
    ).astype(jnp.float32)
    middle = rows_in + live_col * (attn_out + proj_bias_full.astype(jnp.float32))
    gain_two_f = gain_two.astype(jnp.float32)
    shift_two_f = shift_two.astype(jnp.float32)
    fc1_bias_f = fc1_bias_full.astype(jnp.float32)
    norm_two = layer_norm(middle, gain_two_f, shift_two_f).astype(jnp.bfloat16)
    whole_two = lax.all_gather(norm_two, "tensor", axis=0, tiled=True)
    hidden_pre = jnp.dot(whole_two, fc1_full, preferred_element_type=jnp.float32) + fc1_bias_f
    hidden_act = exact_gelu(hidden_pre).astype(jnp.bfloat16)
    row_block = hidden_act
    mlp_out = lax.psum_scatter(
        jnp.dot(row_block, fc2_full, preferred_element_type=jnp.float32).astype(jnp.bfloat16),
        "tensor",
        scatter_dimension=0,
        tiled=True,
    ).astype(jnp.float32)
    result = middle + live_col * (mlp_out + fc2_bias_full.astype(jnp.float32))
    outputs = result.astype(jnp.bfloat16)
    grad_out = cotangent.astype(jnp.float32)
    grad_mlp = (live_col * grad_out).astype(jnp.bfloat16)
    grad_fc2_bias = jnp.sum(grad_mlp, axis=0, dtype=jnp.float32)
    whole_grad_mlp = lax.all_gather(grad_mlp, "tensor", axis=0, tiled=True)
    whole_two = lax.all_gather(norm_two, "tensor", axis=0, tiled=True)
    hidden_pre = jnp.dot(whole_two, fc1_full, preferred_element_type=jnp.float32) + fc1_bias_f
    hidden_act = exact_gelu(hidden_pre).astype(jnp.bfloat16)
    grad_fc2 = contract_rows(hidden_act, whole_grad_mlp)
    grad_act = contract_cols(whole_grad_mlp, fc2_full)
    unused, gelu_pull = jax.vjp(exact_gelu, hidden_pre)
    grad_pre = gelu_pull(grad_act)[0].astype(jnp.bfloat16)
    grad_fc1_bias = jnp.sum(grad_pre, axis=0, dtype=jnp.float32)
    grad_fc1 = contract_rows(whole_two, grad_pre)
    row_block = grad_pre
    grad_two = lax.psum_scatter(
        contract_cols(row_block, fc1_full).astype(jnp.bfloat16),
        "tensor",
        scatter_dimension=0,
        tiled=True,
    ).astype(jnp.float32)
    unused, norm_pull_two = jax.vjp(layer_norm, middle, gain_two_f, shift_two_f)
    grad_mid_norm, grad_gain_two, grad_shift_two = norm_pull_two(grad_two)
    grad_middle = grad_out + grad_mid_norm
    grad_branch = (live_col * grad_middle).astype(jnp.bfloat16)
    grad_proj_bias = jnp.sum(grad_branch, axis=0, dtype=jnp.float32)
    whole_grad_branch = lax.all_gather(grad_branch, "tensor", axis=0, tiled=True)
    grad_proj = contract_rows(mixed_flat, whole_grad_branch)
    grad_mixed = contract_cols(whole_grad_branch, proj_full).astype(jnp.bfloat16)
    grad_mixed_seq = grad_mixed.reshape(slot_count, SEQ_LEN, heads_here, HEAD_DIM)

    def backward_slot(slot_index):
        slot_qkv = lax.dynamic_index_in_dim(packed, slot_index, 1, keepdims=False)
        slot_valid = lax.dynamic_index_in_dim(valid_seq, slot_index, 0, keepdims=False)
        slot_total = lax.dynamic_index_in_dim(log_total, slot_index, 0, keepdims=False)
        slot_grad = lax.dynamic_index_in_dim(grad_mixed_seq, slot_index, 0, keepdims=False)
        return attend_backward(
            slot_qkv[0], slot_qkv[1], slot_qkv[2], slot_valid, slot_total, slot_grad, score_scale
        )

    grad_query, grad_keys, grad_values = lax.map(
        backward_slot, jnp.arange(slot_count, dtype=jnp.int32)
    )
    grad_packed = jnp.stack((grad_query, grad_keys, grad_values)).reshape(3, whole_rows, width_here)
    whole_one = lax.all_gather(norm_one, "tensor", axis=0, tiled=True)
    grad_qkv = jnp.einsum("nd,jnc->jdc", whole_one, grad_packed, preferred_element_type=jnp.float32)
    row_block = grad_packed
    grad_one = lax.psum_scatter(
        jnp.einsum("jnc,jdc->nd", row_block, qkv_full, preferred_element_type=jnp.float32).astype(
            jnp.bfloat16
        ),
        "tensor",
        scatter_dimension=0,
        tiled=True,
    ).astype(jnp.float32)
    unused, norm_pull_one = jax.vjp(layer_norm, rows_in, gain_one_f, shift_one_f)
    grad_in_norm, grad_gain_one, grad_shift_one = norm_pull_one(grad_one)
    grad_inputs = (grad_middle + grad_in_norm).astype(jnp.bfloat16)
    (
        out_qkv,
        out_proj,
        sum_proj_bias,
        sum_gain_one,
        sum_shift_one,
        out_fc1,
        out_fc1_bias,
        out_fc2,
        sum_gain_two,
        sum_shift_two,
        sum_fc2_bias,
    ) = (
        lax.psum_scatter(
            grad_qkv.astype(jnp.bfloat16), "dp", scatter_dimension=1, tiled=True
        ).astype(jnp.float32),
        lax.psum_scatter(
            grad_proj.astype(jnp.bfloat16), "dp", scatter_dimension=1, tiled=True
        ).astype(jnp.float32),
        lax.psum_scatter(
            grad_proj_bias.astype(jnp.bfloat16), "dp", scatter_dimension=0, tiled=True
        ).astype(jnp.float32),
        lax.psum_scatter(
            grad_gain_one.astype(jnp.bfloat16), "dp", scatter_dimension=0, tiled=True
        ).astype(jnp.float32),
        lax.psum_scatter(
            grad_shift_one.astype(jnp.bfloat16), "dp", scatter_dimension=0, tiled=True
        ).astype(jnp.float32),
        lax.psum_scatter(
            grad_fc1.astype(jnp.bfloat16), "dp", scatter_dimension=0, tiled=True
        ).astype(jnp.float32),
        lax.psum_scatter(
            grad_fc1_bias.astype(jnp.bfloat16), "dp", scatter_dimension=0, tiled=True
        ).astype(jnp.float32),
        lax.psum_scatter(
            grad_fc2.astype(jnp.bfloat16), "dp", scatter_dimension=1, tiled=True
        ).astype(jnp.float32),
        lax.psum_scatter(
            grad_gain_two.astype(jnp.bfloat16), "dp", scatter_dimension=0, tiled=True
        ).astype(jnp.float32),
        lax.psum_scatter(
            grad_shift_two.astype(jnp.bfloat16), "dp", scatter_dimension=0, tiled=True
        ).astype(jnp.float32),
        lax.psum_scatter(
            grad_fc2_bias.astype(jnp.bfloat16), "dp", scatter_dimension=0, tiled=True
        ).astype(jnp.float32),
    )
    sum_gain_one, sum_shift_one, sum_proj_bias, sum_gain_two, sum_shift_two, sum_fc2_bias = (
        lax.psum(
            (sum_gain_one, sum_shift_one, sum_proj_bias, sum_gain_two, sum_shift_two, sum_fc2_bias),
            "tensor",
        )
    )
    return (
        outputs,
        grad_inputs,
        sum_gain_one,
        sum_shift_one,
        out_qkv,
        out_proj,
        sum_proj_bias,
        sum_gain_two,
        sum_shift_two,
        out_fc1,
        out_fc1_bias,
        out_fc2,
        sum_fc2_bias,
    )


def solution(mesh):
    in_specs = (
        P(("dp", "tensor"), None),
        P(("dp", "tensor"), None),
        P("dp"),
        P(("dp", "tensor")),
        P("dp"),
        P("dp"),
        P(None, "dp", "tensor"),
        P("tensor", "dp"),
        P("dp"),
        P("dp"),
        P("dp"),
        P("dp", "tensor"),
        P(("tensor", "dp")),
        P("tensor", "dp"),
        P("dp"),
    )
    out_specs = (
        P(("dp", "tensor"), None),
        P(("dp", "tensor"), None),
        P("dp"),
        P("dp"),
        P(None, "dp", "tensor"),
        P("tensor", "dp"),
        P("dp"),
        P("dp"),
        P("dp"),
        P("dp", "tensor"),
        P(("tensor", "dp")),
        P("tensor", "dp"),
        P("dp"),
    )
    return jax.shard_map(
        on_device, mesh=mesh, in_specs=in_specs, out_specs=out_specs, check_vma=False
    )
```

profile of v0, /device:TPU:0, one launch (start us, length us, event | category | flops | bytes accessed | tf_op | source)
XLA Modules:
  0.0 1062.3 jit_solution(11267200392812141874)
XLA Ops:
  13.4 78.6 %all-reduce.17 = (bf16[1024]{0:T(1024)(128)(2,1)S(1)}, bf16[1024]{0:T(1024)(128)(2,1)S(1)}, bf16[1024]{0:T(1024)(128)(2,1)S(1)}, bf16[1024]{0:T(1024)(128)(2,1)S(1)}, bf16[1024]{0:T(1024)(128)(2,1)S(1)}) all-reduce(bf16[1024]{0:T(1024)(128)(2,1)S(1)} %dynamic-update-slice.5, ...), channel_id=1, replica_groups=mesh['dp'=16,'tensor'=2] {'dp'}, use_global_device_ids=true, to_apply=%add.5 | all-reduce | flops 5120 | bytes 20480
  101.0 2.7 all-reduce.2
  104.8 71.6 %all-gather.12.cloned.1.call-done = bf16[3,1024,512]{2,1,0:T(8,128)(2,1)} async-done(((bf16[3,64,512]{2,1,0:T(8,128)(2,1)}), bf16[3,1024,512]{2,1,0:T(8,128)(2,1)}) %all-gather.12.cloned.1.call-update) | async-done | bytes 3145744 | tf_op jit(solution)/shard_map/all_gather | solution.py:121
  176.4 6.2 fusion.13
  185.0 2.1 copy.57
  187.1 2.8 copy.56
  190.0 15.7 %fusion.55 = (f32[8,1104]{1,0:T(8,128)S(1)}, f32[8,1104,1104]{1,2,0:T(8,128)}) fusion(bf16[1104,8,64]{0,2,1:T(8,128)(2,1)S(1)} %bitcast.65, bf16[1104,8,64]{0,2,1:T(8,128)(2,1)S(1)} %bitcast.67, pred[1104]{0:T(1024)(128)(4,1)S(1)} %broadcast_compare_fusion), kind=kOutput, calls=%fused_computation.120 | convolution fusion | flops 1277310336 | bytes 41299536 | tf_op jit(solution)/shard_map/while/body/eval_jaxpr/qhd,khd->hqk/dot_general | solution.py:23
  205.7 16.2 %fusion.1 = f32[8,1104]{1,0:T(8,128)S(1)} fusion(f32[8,1104,1104]{1,2,0:T(8,128)} %get-tuple-element.131, f32[8,1104]{1,0:T(8,128)S(1)} %get-tuple-element.130), kind=kLoop, calls=%fused_computation.7 | loop fusion | flops 19492224 | bytes 39072768 | tf_op jit(solution)/shard_map/while/body/eval_jaxpr/reduce_sum | solution.py:32
  221.9 15.8 %fusion.23 = bf16[8,64,1104]{2,1,0:T(8,128)(2,1)S(1)} fusion(bf16[1104,8,64]{0,2,1:T(8,128)(2,1)S(1)} %bitcast.69, f32[8,1104,1104]{1,2,0:T(8,128)} %get-tuple-element.131, f32[8,1104]{1,0:T(8,128)S(1)} %fusion.1, f32[8,1104]{1,0:T(8,128)S(1)} %get-tuple-element.130), kind=kOutput, calls=%fused_computation.55 | convolution fusion | flops 1277884416 | bytes 41333760 | tf_op jit(solution)/shard_map/while/body/eval_jaxpr/hqk,khd->qhd/dot_general | solution.py:34
  237.8 4.5 convolution_convert_fusion.1
  244.2 7.2 reduce-scatter.8.cloned.1.call-done
  251.4 1.9 fusion.46
  256.0 1.9 fusion.49
  258.7 40.7 %all-gather = bf16[16,1,128]{2,1,0:T(2,128)(2,1)S(1)} all-gather(bf16[1,1,128]{2,1,0:T(2,128)(2,1)S(1)} %bitcast.75), channel_id=1, replica_groups=mesh['dp'=16,'tensor'=2] {'dp'}, dimensions={0}, use_global_device_ids=true | all-gather | bytes 4352 | tf_op jit(solution)/shard_map/all_gather | solution.py:127
  299.4 31.8 %all-gather.18.cloned.1.call-done = bf16[1024,2048]{1,0:T(8,128)(2,1)} async-done(((bf16[64,2048]{1,0:T(8,128)(2,1)}), bf16[1024,2048]{1,0:T(8,128)(2,1)}) %all-gather.18.cloned.1.call-update) | async-done | bytes 4194320 | tf_op jit(solution)/shard_map/all_gather | solution.py:126
  331.2 11.4 %all-gather.16.cloned.1.call-done = bf16[1104,1024]{1,0:T(8,128)(2,1)} async-done(((bf16[552,1024]{1,0:T(8,128)(2,1)}), bf16[1104,1024]{1,0:T(8,128)(2,1)}) %all-gather.16.cloned.1.call-update) | async-done | bytes 2261008 | tf_op jit(solution)/shard_map/all_gather | solution.py:164
  342.6 11.6 %convolution_add_fusion = f32[1104,2048]{1,0:T(8,128)} fusion(bf16[1104,1024]{1,0:T(8,128)(2,1)} %all-gather.16.cloned.1.call-done, bf16[1024,2048]{1,0:T(8,128)(2,1)} %all-gather.18.cloned.1.call-done, f32[2048]{0:T(1024)S(1)} %bitcast.74), kind=kOutput, calls=%fused_computation.13 | convolution fusion | flops 4632772608 | bytes 15507456 | tf_op jit(solution)/shard_map/dot_general | solution.py:165
  354.2 2.6 all-gather.22.cloned.1.call-done
  356.8 80.1 %all-gather.20.cloned.1.call-done = bf16[2048,1024]{0,1:T(8,128)(2,1)} async-done(((bf16[2048,64]{0,1:T(8,128)(2,1)}), bf16[2048,1024]{0,1:T(8,128)(2,1)}) %all-gather.20.cloned.1.call-update) | async-done | bytes 4194320 | tf_op jit(solution)/shard_map/all_gather | solution.py:128
  436.8 29.1 %fusion.47 = (bf16[2048]{0:T(1024)(128)(2,1)}, bf16[1104,2048]{1,0:T(8,128)(2,1)S(1)}, f32[1104,2048]{1,0:T(8,128)}) fusion(f32[1104,2048]{1,0:T(8,128)} %convolution_add_fusion, bf16[1104,1024]{1,0:T(8,128)(2,1)} %all-gather.22.cloned.1.call-done, bf16[2048,1024]{0,1:T(8,128)(2,1)} %all-gather.20.cloned.1.call-done), kind=kOutput, calls=%fused_computation.114 | convolution fusion | flops 4795561984 | bytes 29069312 | tf_op jit(solution)/shard_map/dot_general | solution.py:72
  466.0 2.1 copy-done.45
  468.1 6.2 convolution_convert_fusion.4
  474.5 8.3 reduce-scatter.12.cloned.1.call-done
  482.8 3.3 fusion.32
  487.4 2.3 fusion.51
  489.8 10.7 %multiply_convert_fusion.1 = bf16[1104,2048]{1,0:T(8,128)(2,1)} fusion(f32[1104,2048]{1,0:T(8,128)} %get-tuple-element.116, f32[1104,2048]{1,0:T(8,128)} %convolution_add_fusion), kind=kLoop, calls=%fused_computation.16 | loop fusion | flops 6782976 | bytes 22609920 | tf_op jit(solution)/shard_map/convert_element_type | solution.py:166
  500.5 9.5 convolution_convert_fusion.2
  511.7 9.5 convolution_convert_fusion.3
  522.4 3.0 convolution_convert_fusion.6
  526.1 16.6 %fusion.20 = bf16[8,64,1104]{2,1,0:T(8,128)(2,1)} fusion(bf16[1104,8,64]{0,2,1:T(8,128)(2,1)S(1)} %bitcast.63, f32[8,1104,1104]{1,2,0:T(8,128)} %get-tuple-element.131, f32[8,1104]{1,0:T(8,128)S(1)} %log_add_fusion), kind=kOutput, calls=%fused_computation.53 | convolution fusion | flops 1268133888 | bytes 41298432 | tf_op jit(solution)/shard_map/while/body/eval_jaxpr/hqk,qhd->khd/dot_general | solution.py:52
  542.7 30.0 %multiply_reduce_fusion = (f32[8,1104]{1,0:T(8,128)S(1)}, f32[8,1104,1104]{1,2,0:T(8,128)}) fusion(f32[8,1104,1104]{1,2,0:T(8,128)} %get-tuple-element.131, f32[8,1104]{1,0:T(8,128)S(1)} %log_add_fusion, bf16[1104,8,64]{0,2,1:T(8,128)(2,1)S(1)} %bitcast.64, bf16[1104,8,64]{0,2,1:T(8,128)(2,1)S(1)} %bitcast.70), kind=kOutput, calls=%fused_computation.3 | convolution fusion | flops 1277310336 | bytes 80335872 | tf_op jit(solution)/shard_map/while/body/eval_jaxpr/qhd,khd->hqk/dot_general | solution.py:41
  572.7 2.3 copy.66
  575.0 33.6 %multiply_convert_fusion = bf16[8,1104,1104]{1,2,0:T(8,128)(2,1)} fusion(f32[8,1104,1104]{1,2,0:T(8,128)} %get-tuple-element.133, f32[8,1104,1104]{1,2,0:T(8,128)} %get-tuple-element.131, f32[8,1104]{1,0:T(8,128)S(1)} %get-tuple-element.132, f32[8,1104]{1,0:T(8,128)S(1)} %log_add_fusion), kind=kLoop, calls=%fused_computation.2 | loop fusion | flops 39002112 | bytes 97575936 | tf_op jit(solution)/shard_map/while/body/eval_jaxpr/convert_element_type | solution.py:43
  608.6 10.4 fusion.18
  620.4 4.6 convolution_convert_fusion.7
  625.6 10.3 fusion.19
  637.9 8.0 convert_bitcast_fusion
  645.9 7.6 copy.67
  654.8 6.8 bitcast_convert_fusion
  661.9 9.8 convolution_convert_fusion.5
  675.5 27.9 %reduce-scatter.18.cloned.1.call-done = bf16[64,2048]{1,0:T(8,128)(2,1)} async-done(((bf16[1024,2048]{1,0:T(8,128)(2,1)}), bf16[64,2048]{1,0:T(8,128)(2,1)}) %reduce-scatter.18.cloned.1.call-update) | async-done | bytes 262160 | tf_op jit(solution)/shard_map/reduce_scatter | solution.py:261
  705.2 77.7 %reduce-scatter.16.cloned.1.call-done = bf16[512,64]{0,1:T(8,128)(2,1)} async-done(((bf16[512,1024]{0,1:T(8,128)(2,1)}), bf16[512,64]{0,1:T(8,128)(2,1)}) %reduce-scatter.16.cloned.1.call-update) | async-done | bytes 65552 | tf_op jit(solution)/shard_map/reduce_scatter | solution.py:249
  784.4 169.8 %all-reduce.20.cloned.1.call-done = bf16[3,1024,512]{2,0,1:T(4,128)(2,1)} async-done(((bf16[3,1024,512]{2,0,1:T(4,128)(2,1)}), bf16[3,1024,512]{2,0,1:T(4,128)(2,1)}) %all-reduce.20.cloned.1.call-update) | async-done | bytes 3145744
  956.1 9.0 reduce-scatter.14.cloned.1.call-done
  966.8 1.9 fusion.35
  970.1 77.0 %all-reduce.16 = (bf16[1024]{0:T(1024)(128)(2,1)S(1)}, bf16[1024]{0:T(1024)(128)(2,1)S(1)}, bf16[1024]{0:T(1024)(128)(2,1)S(1)}, bf16[1024]{0:T(1024)(128)(2,1)S...) all-reduce(bf16[1024]{0:T(1024)(128)(2,1)S(1)} %dynamic-update-slic, ...), channel_id=1, replica_groups=mesh['dp'=16,'tensor'=2] {'dp'}, use_global_device_ids=true, to_apply=%add.6 | all-reduce | flops 9216 | bytes 36864
  1047.4 3.0 all-reduce.15
  1051.0 4.6 add_convert_fusion.1
  (186 shorter events, 43.6 us)
Async XLA Ops:
  7.2 89.3 %copy-start = (bf16[552,1024]{1,0:T(8,128)(2,1)S(1)}, bf16[552,1024]{1,0:T(8,128)(2,1)}, u32[]{:S(2)}) copy-start(bf16[552,1024]{1,0:T(8,128)(2,1)} %param.15) | copy-start | bytes 3391492
  7.2 97.6 %all-gather.10.cloned.1.call-start = ((), (), s32[]{:S(2)}) async-start(), calls=%async_computation.7 | async-start | bytes 3391488 | tf_op jit(solution)/shard_map/all_gather | solution.py:138
  92.0 3.8 copy-start.24
  93.5 6.0 copy-start.44
  93.5 6.6 copy-start.35
  98.0 78.4 %all-gather.12.cloned.1.call-start = ((), (), s32[]{:S(2)}) async-start(), calls=%async_computation.8 | async-start | bytes 3342336 | tf_op jit(solution)/shard_map/all_gather | solution.py:121
  98.7 139.1 %all-gather.14.cloned.1.call-start = ((), (), s32[]{:S(2)}) async-start(), calls=%async_computation.9 | async-start | bytes 1114112 | tf_op jit(solution)/shard_map/all_gather | solution.py:122
  99.4 152.0 %reduce-scatter.8.cloned.1.call-start = ((), (), s32[]{:S(2)}) async-start(), calls=%async_computation.10 | async-start | bytes 3391488 | tf_op jit(solution)/shard_map/reduce_scatter | solution.py:153
  185.0 5.0 copy-start.8
  187.1 18.6 %copy-start.6 = (bf16[1,1104,512]{1,2,0:T(8,128)(2,1)}, bf16[1,1104,512]{1,2,0:T(8,128)(2,1)S(1)}, u32[]{:S(2)}) copy-start(bf16[1,1104,512]{1,2,0:T(8,128)(2,1)S(1)} %copy.57) | copy-start | bytes 3391492
  205.7 16.2 %copy-start.13 = (bf16[1,1104,512]{1,2,0:T(8,128)(2,1)S(1)}, bf16[1,1104,512]{1,2,0:T(8,128)(2,1)}, u32[]{:S(2)}) copy-start(bf16[1,1104,512]{1,2,0:T(8,128)(2,1)} %copy.56) | copy-start | bytes 3391492
  237.7 4.5 copy-start.43
  242.3 88.9 %all-gather.18.cloned.1.call-start = ((), (), s32[]{:S(2)}) async-start(), calls=%async_computation.12 | async-start | bytes 4456448 | tf_op jit(solution)/shard_map/all_gather | solution.py:126
  242.9 99.8 %all-gather.16.cloned.1.call-start = ((), (), s32[]{:S(2)}) async-start(), calls=%async_computation.11 | async-start | bytes 3391488 | tf_op jit(solution)/shard_map/all_gather | solution.py:164
  244.1 242.0 %copy-start.20 = (f32[1024]{0:T(1024)}, f32[1024]{0:T(1024)S(1)}, u32[]{:S(2)}) copy-start(f32[1024]{0:T(1024)S(1)} %convert_element_type.206) | copy-start | bytes 12292
  244.2 243.2 %copy-start.18 = (f32[552]{0:T(1024)}, f32[552]{0:T(1024)S(1)}, u32[]{:S(2)}) copy-start(f32[552]{0:T(1024)S(1)} %fusion.40) | copy-start | bytes 6628
  255.9 2.8 copy-start.37
  255.9 100.9 %all-gather.22.cloned.1.call-start = ((), (), s32[]{:S(2)}) async-start(), calls=%async_computation.15 | async-start | bytes 3391488 | tf_op jit(solution)/shard_map/all_gather | solution.py:179
  257.9 178.9 %all-gather.20.cloned.1.call-start = ((), (), s32[]{:S(2)}) async-start(), calls=%async_computation.13 | async-start | bytes 4456448 | tf_op jit(solution)/shard_map/all_gather | solution.py:128
  258.7 224.2 %reduce-scatter.12.cloned.1.call-start = ((), (), s32[]{:S(2)}) async-start(), calls=%async_computation.16 | async-start | bytes 3391488 | tf_op jit(solution)/shard_map/reduce_scatter | solution.py:190
  436.8 31.2 %copy-start.38 = (bf16[1024,2048]{1,0:T(8,128)(2,1)S(1)}, bf16[1024,2048]{1,0:T(8,128)(2,1)}, u32[]{:S(2)}) copy-start(bf16[1024,2048]{1,0:T(8,128)(2,1)} %all-gather.18.cloned.1.call-done) | copy-start | bytes 12582916
  474.3 47.2 %all-gather.24.cloned.1.call-start = ((), (), s32[]{:S(2)}) async-start(), calls=%async_computation.17 | async-start | bytes 3391488 | tf_op jit(solution)/shard_map/all_gather | solution.py:201
  482.8 3.3 copy-start.11
  487.4 2.3 copy-start.4
  489.8 183.9 %reduce-scatter.20.cloned.1.call-start = ((), (), s32[]{:S(2)}) async-start(), calls=%async_computation.21 | async-start | bytes 4456448 | tf_op jit(solution)/shard_map/reduce_scatter | solution.py:267
  489.8 10.7 %copy-start.40 = (bf16[1104,1024]{1,0:T(8,128)(2,1)S(1)}, bf16[1104,1024]{1,0:T(8,128)(2,1)}, u32[]{:S(2)}) copy-start(bf16[1104,1024]{1,0:T(8,128)(2,1)} %all-gather.22.cloned.1.call-done) | copy-start | bytes 6782980
  510.1 193.3 %reduce-scatter.18.cloned.1.call-start = ((), (), s32[]{:S(2)}) async-start(), calls=%async_computation.20 | async-start | bytes 4456448 | tf_op jit(solution)/shard_map/reduce_scatter | solution.py:261
  521.2 261.7 %reduce-scatter.16.cloned.1.call-start = ((), (), s32[]{:S(2)}) async-start(), calls=%async_computation.19 | async-start | bytes 1114112 | tf_op jit(solution)/shard_map/reduce_scatter | solution.py:249
  526.1 16.6 %copy-start.14 = (bf16[1,1104,512]{1,2,0:T(8,128)(2,1)S(1)}, bf16[1,1104,512]{1,2,0:T(8,128)(2,1)}, u32[]{:S(2)}) copy-start(bf16[1,1104,512]{1,2,0:T(8,128)(2,1)} %copy.56) | copy-start | bytes 3391492
  575.0 33.6 %copy-start.9 = (bf16[1,1104,512]{1,2,0:T(8,128)(2,1)S(1)}, bf16[1,1104,512]{1,2,0:T(8,128)(2,1)}, u32[]{:S(2)}) copy-start(bf16[1,1104,512]{1,2,0:T(8,128)(2,1)} %copy-done.8) | copy-start | bytes 3391492
  620.4 5.1 copy-start.7
  625.1 329.2 %all-reduce.20.cloned.1.call-start = ((), (), s32[]{:S(2)}) async-start(), calls=%async_computation.22 | async-start | bytes 8388608
  653.5 311.6 %reduce-scatter.14.cloned.1.call-start = ((), (), s32[]{:S(2)}) async-start(), calls=%async_computation.18 | async-start | bytes 3391488 | tf_op jit(solution)/shard_map/reduce_scatter | solution.py:222
  661.6 389.3 %reduce-scatter.10.cloned.1.call-start = ((), (), s32[]{:S(2)}) async-start(), calls=%async_computation.14 | async-start | bytes 3391488 | tf_op jit(solution)/shard_map/reduce_scatter | solution.py:168
  673.6 293.1 %copy-start.1 = (bf16[552,1024]{1,0:T(8,128)(2,1)S(1)}, bf16[552,1024]{1,0:T(8,128)(2,1)}, u32[]{:S(2)}) copy-start(bf16[552,1024]{1,0:T(8,128)(2,1)} %param.15) | copy-start | bytes 3391492
  673.6 293.1 %copy-start.23 = (f32[552]{0:T(1024)S(1)}, f32[552]{0:T(1024)}, u32[]{:S(2)}) copy-start(f32[552]{0:T(1024)} %copy-done.22) | copy-start | bytes 6628
  673.6 293.1 %copy-start.25 = (f32[1024]{0:T(1024)S(1)}, f32[1024]{0:T(1024)}, u32[]{:S(2)}) copy-start(f32[1024]{0:T(1024)} %copy-done.24) | copy-start | bytes 12292
  955.2 13.5 %copy-start.29 = (f32[552]{0:T(1024)S(1)}, f32[552]{0:T(1024)}, u32[]{:S(2)}) copy-start(f32[552]{0:T(1024)} %copy-done.28) | copy-start | bytes 6628
  955.3 13.5 %copy-start.27 = (f32[552]{0:T(1024)S(1)}, f32[552]{0:T(1024)}, u32[]{:S(2)}) copy-start(f32[552]{0:T(1024)} %copy-done.26) | copy-start | bytes 6628
  965.2 3.6 copy-start.5
  966.7 3.4 copy-start.32
  966.8 3.4 copy-start.33
  966.8 3.4 copy-start.34
  966.8 3.4 copy-start.36
  966.8 84.1 %copy-start.3 = (bf16[552,1024]{1,0:T(8,128)(2,1)S(1)}, bf16[552,1024]{1,0:T(8,128)(2,1)}, u32[]{:S(2)}) copy-start(bf16[552,1024]{1,0:T(8,128)(2,1)} %reduce-scatter.8.cloned.1.call-done) | copy-start | bytes 3391492
  966.8 84.1 %copy-start.19 = (f32[552]{0:T(1024)S(1)}, f32[552]{0:T(1024)}, u32[]{:S(2)}) copy-start(f32[552]{0:T(1024)} %copy-done.18) | copy-start | bytes 6628
  966.8 84.1 %copy-start.21 = (f32[1024]{0:T(1024)S(1)}, f32[1024]{0:T(1024)}, u32[]{:S(2)}) copy-start(f32[1024]{0:T(1024)} %copy-done.20) | copy-start | bytes 12292
  966.8 84.1 %copy-start.31 = (f32[552]{0:T(1024)S(1)}, f32[552]{0:T(1024)}, u32[]{:S(2)}) copy-start(f32[552]{0:T(1024)} %copy-done.30) | copy-start | bytes 6628
  (14 other events, 22.4 us)
Sparse Core Ops, SparseCore 0:
  98.1 6.6 all-gather.9
  107.6 68.7 all-gather.11
  179.1 54.3 all-gather.13
  242.4 8.9 reduce-scatter.7
  254.0 77.1 all-gather.17
  333.2 9.4 all-gather.15
  344.8 11.9 all-gather.21
  359.6 77.2 all-gather.19
  474.4 8.3 reduce-scatter.11
  489.9 11.9 all-gather.23
  510.2 96.2 reduce-scatter.19
  608.6 94.7 reduce-scatter.17
  705.7 77.2 reduce-scatter.15
  789.3 164.8 all-reduce.19
  956.4 8.7 reduce-scatter.13
  967.3 10.9 reduce-scatter.9
where the time goes:
time: 1070 us; the launch traced here: 1060 us
  waiting for transfers between devices  501 us (47%)
  matrix products  208 us (19%)
  blocking collectives  202 us (19%)
  other arithmetic  95 us (9%)
  local copies, waits for them, and re-layouts  36 us (3%)
  between operations  18.1 us (2%)
    unnamed x17, waiting for transfers between devices  173 us
    unnamed x3, blocking collectives  158 us
    all_gather x1, waiting for transfers between devices, on_device(): lax.all_gather(fc2_weight, 'dp', axis=1, tiled=True)  80.1 us
    reduce_scatter x1, waiting for transfers between devices, on_device(): lax.psum_scatter(grad_proj.astype(jnp.bfloat16), 'dp', scatter_dimension=...  77.7 us
    all_gather x1, waiting for transfers between devices, on_device(): lax.all_gather(qkv_weight, 'dp', axis=1, tiled=True)  71.6 us
    all_gather x1, blocking collectives, on_device(): lax.all_gather(fc1_bias, 'dp', axis=0, tiled=True)  40.7 us
    dot_general x3, matrix products, contract_cols(): lax.dot_general(left, right, (((1,), (1,)), ((), ())), preferred_element_...  38.3 us
    convert_element_type x1, other arithmetic, attend_backward(): grad_scores = (attn_prob * (grad_prob - row_dot)).astype(jnp.bfloat16)  33.6 us
  transfers between devices with their start and end apart: 16, of which 12 were waited for; matrix products, arithmetic and copies ran while one was open for 25% of the time, Pallas kernels for 0%

commit v1 on v0

--- a/solution.py
+++ b/solution.py
@@ -124,7 +124,9 @@
         lax.all_gather(attn_norm_gain, "dp", axis=0, tiled=True),
         lax.all_gather(attn_norm_bias, "dp", axis=0, tiled=True),
         lax.all_gather(fc1_weight, "dp", axis=0, tiled=True),
-        lax.all_gather(fc1_bias, "dp", axis=0, tiled=True),
+        jnp.concatenate(
+            lax.all_to_all(jnp.stack([fc1_bias] * lax.axis_size("dp")), "dp", 0, 0), axis=0
+        ),
         lax.all_gather(fc2_weight, "dp", axis=1, tiled=True),
         lax.all_gather(mlp_norm_gain, "dp", axis=0, tiled=True),
         lax.all_gather(mlp_norm_bias, "dp", axis=0, tiled=True),

time: 1070 us -> 1070 us (level)
  blocking collectives: 202 us -> 175 us
  waiting for transfers between devices: 501 us -> 528 us
    all_gather x1 -> x0, blocking collectives: 40.7 us -> none  [on_device(): lax.all_gather(fc1_bias, 'dp', axis=0, tiled=True)]
    all_gather x1, waiting for transfers between devices: 31.8 us -> 58.8 us  [on_device(): lax.all_gather(fc1_weight, 'dp', axis=0, tiled=True)]
    all_to_all x0 -> x1, blocking collectives: none -> 13.8 us  [on_device(): lax.all_to_all(jnp.stack([fc1_bias] * lax.axis_size('dp')), 'dp', 0, 0)]
where the time goes in v1:
time: 1070 us; the launch traced here: 1060 us
  waiting for transfers between devices  528 us (49%)
  matrix products  208 us (19%)
  blocking collectives  175 us (16%)
  other arithmetic  95 us (9%)
  local copies, waits for them, and re-layouts  36 us (3%)
  between operations  18.2 us (2%)
    unnamed x17, waiting for transfers between devices  173 us
    unnamed x3, blocking collectives  158 us
    all_gather x1, waiting for transfers between devices, on_device(): lax.all_gather(fc2_weight, 'dp', axis=1, tiled=True)  80.1 us
    reduce_scatter x1, waiting for transfers between devices, on_device(): lax.psum_scatter(grad_proj.astype(jnp.bfloat16), 'dp', scatter_dimension=...  77.7 us
    all_gather x1, waiting for transfers between devices, on_device(): lax.all_gather(qkv_weight, 'dp', axis=1, tiled=True)  71.6 us
    all_gather x1, waiting for transfers between devices, on_device(): lax.all_gather(fc1_weight, 'dp', axis=0, tiled=True)  58.8 us
    dot_general x3, matrix products, contract_cols(): lax.dot_general(left, right, (((1,), (1,)), ((), ())), preferred_element_...  38.3 us
    convert_element_type x1, other arithmetic, attend_backward(): grad_scores = (attn_prob * (grad_prob - row_dot)).astype(jnp.bfloat16)  33.6 us
  transfers between devices with their start and end apart: 16, of which 12 were waited for; matrix products, arithmetic and copies ran while one was open for 25% of the time, Pallas kernels for 0%

profile of v1, /device:TPU:0, one launch (start us, length us, event | category | flops | bytes accessed | tf_op | source)
XLA Modules:
  0.0 1062.4 jit_solution(2529646889940063638)
XLA Ops:
  13.4 78.6 %all-reduce.17 = (bf16[1024]{0:T(1024)(128)(2,1)S(1)}, bf16[1024]{0:T(1024)(128)(2,1)S(1)}, bf16[1024]{0:T(1024)(128)(2,1)S(1)}, bf16[1024]{0:T(1024)(128)(2,1)S(1)}, bf16[1024]{0:T(1024)(128)(2,1)S(1)}) all-reduce(bf16[1024]{0:T(1024)(128)(2,1)S(1)} %dynamic-update-slice.5, ...), channel_id=1, replica_groups=mesh['dp'=16,'tensor'=2] {'dp'}, use_global_device_ids=true, to_apply=%add.5 | all-reduce | flops 5120 | bytes 20480
  101.0 2.7 all-reduce.2
  104.8 71.6 %all-gather.11.cloned.1.call-done = bf16[3,1024,512]{2,1,0:T(8,128)(2,1)} async-done(((bf16[3,64,512]{2,1,0:T(8,128)(2,1)}), bf16[3,1024,512]{2,1,0:T(8,128)(2,1)}) %all-gather.11.cloned.1.call-update) | async-done | bytes 3145744 | tf_op jit(solution)/shard_map/all_gather | solution.py:121
  176.4 6.2 fusion.13
  185.0 2.1 copy.57
  187.1 2.8 copy.56
  190.0 15.7 %fusion.55 = (f32[8,1104]{1,0:T(8,128)S(1)}, f32[8,1104,1104]{1,2,0:T(8,128)}) fusion(bf16[1104,8,64]{0,2,1:T(8,128)(2,1)S(1)} %bitcast.64, bf16[1104,8,64]{0,2,1:T(8,128)(2,1)S(1)} %bitcast.66, pred[1104]{0:T(1024)(128)(4,1)S(1)} %broadcast_compare_fusion), kind=kOutput, calls=%fused_computation.120 | convolution fusion | flops 1277310336 | bytes 41299536 | tf_op jit(solution)/shard_map/while/body/eval_jaxpr/qhd,khd->hqk/dot_general | solution.py:23
  205.7 16.2 %fusion.1 = f32[8,1104]{1,0:T(8,128)S(1)} fusion(f32[8,1104,1104]{1,2,0:T(8,128)} %get-tuple-element.131, f32[8,1104]{1,0:T(8,128)S(1)} %get-tuple-element.130), kind=kLoop, calls=%fused_computation.7 | loop fusion | flops 19492224 | bytes 39072768 | tf_op jit(solution)/shard_map/while/body/eval_jaxpr/reduce_sum | solution.py:32
  221.9 15.8 %fusion.23 = bf16[8,64,1104]{2,1,0:T(8,128)(2,1)S(1)} fusion(bf16[1104,8,64]{0,2,1:T(8,128)(2,1)S(1)} %bitcast.68, f32[8,1104,1104]{1,2,0:T(8,128)} %get-tuple-element.131, f32[8,1104]{1,0:T(8,128)S(1)} %fusion.1, f32[8,1104]{1,0:T(8,128)S(1)} %get-tuple-element.130), kind=kOutput, calls=%fused_computation.55 | convolution fusion | flops 1277884416 | bytes 41333760 | tf_op jit(solution)/shard_map/while/body/eval_jaxpr/hqk,khd->qhd/dot_general | solution.py:34
  237.8 4.5 convolution_convert_fusion.1
  244.2 7.2 reduce-scatter.8.cloned.1.call-done
  251.4 1.9 fusion.46
  256.0 1.9 fusion.49
  258.7 13.8 %all_to_all.6 = bf16[16,1,128]{2,1,0:T(2,128)(2,1)S(1)} all-to-all(bf16[16,1,128]{2,1,0:T(2,128)(2,1)S(1)} %stack.10), channel_id=1, replica_groups=mesh['dp'=16,'tensor'=2] {'dp'}, dimensions={0} | all-to-all | bytes 8192 | tf_op jit(solution)/shard_map/all_to_all | solution.py:128
  272.6 58.8 %all-gather.17.cloned.1.call-done = bf16[1024,2048]{1,0:T(8,128)(2,1)} async-done(((bf16[64,2048]{1,0:T(8,128)(2,1)}), bf16[1024,2048]{1,0:T(8,128)(2,1)}) %all-gather.17.cloned.1.call-update) | async-done | bytes 4194320 | tf_op jit(solution)/shard_map/all_gather | solution.py:126
  331.3 11.4 %all-gather.15.cloned.1.call-done = bf16[1104,1024]{1,0:T(8,128)(2,1)} async-done(((bf16[552,1024]{1,0:T(8,128)(2,1)}), bf16[1104,1024]{1,0:T(8,128)(2,1)}) %all-gather.15.cloned.1.call-update) | async-done | bytes 2261008 | tf_op jit(solution)/shard_map/all_gather | solution.py:166
  342.7 11.6 %convolution_add_fusion = f32[1104,2048]{1,0:T(8,128)} fusion(bf16[1104,1024]{1,0:T(8,128)(2,1)} %all-gather.15.cloned.1.call-done, bf16[1024,2048]{1,0:T(8,128)(2,1)} %all-gather.17.cloned.1.call-done, f32[2048]{0:T(1024)S(1)} %bitcast.73), kind=kOutput, calls=%fused_computation.13 | convolution fusion | flops 4632772608 | bytes 15507456 | tf_op jit(solution)/shard_map/dot_general | solution.py:167
  354.3 2.6 all-gather.21.cloned.1.call-done
  356.9 80.1 %all-gather.19.cloned.1.call-done = bf16[2048,1024]{0,1:T(8,128)(2,1)} async-done(((bf16[2048,64]{0,1:T(8,128)(2,1)}), bf16[2048,1024]{0,1:T(8,128)(2,1)}) %all-gather.19.cloned.1.call-update) | async-done | bytes 4194320 | tf_op jit(solution)/shard_map/all_gather | solution.py:130
  436.9 29.1 %fusion.47 = (bf16[2048]{0:T(1024)(128)(2,1)}, bf16[1104,2048]{1,0:T(8,128)(2,1)S(1)}, f32[1104,2048]{1,0:T(8,128)}) fusion(f32[1104,2048]{1,0:T(8,128)} %convolution_add_fusion, bf16[1104,1024]{1,0:T(8,128)(2,1)} %all-gather.21.cloned.1.call-done, bf16[2048,1024]{0,1:T(8,128)(2,1)} %all-gather.19.cloned.1.call-done), kind=kOutput, calls=%fused_computation.114 | convolution fusion | flops 4795561984 | bytes 29069312 | tf_op jit(solution)/shard_map/dot_general | solution.py:72
  466.1 2.1 copy-done.45
  468.2 6.2 convolution_convert_fusion.4
  474.6 8.3 reduce-scatter.12.cloned.1.call-done
  482.9 3.3 fusion.32
  487.5 2.3 fusion.51
  489.9 10.7 %multiply_convert_fusion.1 = bf16[1104,2048]{1,0:T(8,128)(2,1)} fusion(f32[1104,2048]{1,0:T(8,128)} %get-tuple-element.116, f32[1104,2048]{1,0:T(8,128)} %convolution_add_fusion), kind=kLoop, calls=%fused_computation.16 | loop fusion | flops 6782976 | bytes 22609920 | tf_op jit(solution)/shard_map/convert_element_type | solution.py:168
  500.6 9.5 convolution_convert_fusion.2
  511.8 9.5 convolution_convert_fusion.3
  522.5 3.0 convolution_convert_fusion.6
  526.2 16.6 %fusion.20 = bf16[8,64,1104]{2,1,0:T(8,128)(2,1)} fusion(bf16[1104,8,64]{0,2,1:T(8,128)(2,1)S(1)} %bitcast.62, f32[8,1104,1104]{1,2,0:T(8,128)} %get-tuple-element.131, f32[8,1104]{1,0:T(8,128)S(1)} %log_add_fusion), kind=kOutput, calls=%fused_computation.53 | convolution fusion | flops 1268133888 | bytes 41298432 | tf_op jit(solution)/shard_map/while/body/eval_jaxpr/hqk,qhd->khd/dot_general | solution.py:52
  542.8 30.0 %multiply_reduce_fusion = (f32[8,1104]{1,0:T(8,128)S(1)}, f32[8,1104,1104]{1,2,0:T(8,128)}) fusion(f32[8,1104,1104]{1,2,0:T(8,128)} %get-tuple-element.131, f32[8,1104]{1,0:T(8,128)S(1)} %log_add_fusion, bf16[1104,8,64]{0,2,1:T(8,128)(2,1)S(1)} %bitcast.63, bf16[1104,8,64]{0,2,1:T(8,128)(2,1)S(1)} %bitcast.69), kind=kOutput, calls=%fused_computation.3 | convolution fusion | flops 1277310336 | bytes 80335872 | tf_op jit(solution)/shard_map/while/body/eval_jaxpr/qhd,khd->hqk/dot_general | solution.py:41
  572.8 2.3 copy.66
  575.1 33.6 %multiply_convert_fusion = bf16[8,1104,1104]{1,2,0:T(8,128)(2,1)} fusion(f32[8,1104,1104]{1,2,0:T(8,128)} %get-tuple-element.133, f32[8,1104,1104]{1,2,0:T(8,128)} %get-tuple-element.131, f32[8,1104]{1,0:T(8,128)S(1)} %get-tuple-element.132, f32[8,1104]{1,0:T(8,128)S(1)} %log_add_fusion), kind=kLoop, calls=%fused_computation.2 | loop fusion | flops 39002112 | bytes 97575936 | tf_op jit(solution)/shard_map/while/body/eval_jaxpr/convert_element_type | solution.py:43
  608.7 10.4 fusion.18
  620.5 4.6 convolution_convert_fusion.7
  625.7 10.3 fusion.19
  638.0 8.0 convert_bitcast_fusion
  646.0 7.6 copy.67
  654.9 6.8 bitcast_convert_fusion
  662.0 9.8 convolution_convert_fusion.5
  675.6 27.9 %reduce-scatter.18.cloned.1.call-done = bf16[64,2048]{1,0:T(8,128)(2,1)} async-done(((bf16[1024,2048]{1,0:T(8,128)(2,1)}), bf16[64,2048]{1,0:T(8,128)(2,1)}) %reduce-scatter.18.cloned.1.call-update) | async-done | bytes 262160 | tf_op jit(solution)/shard_map/reduce_scatter | solution.py:263
  705.3 77.7 %reduce-scatter.16.cloned.1.call-done = bf16[512,64]{0,1:T(8,128)(2,1)} async-done(((bf16[512,1024]{0,1:T(8,128)(2,1)}), bf16[512,64]{0,1:T(8,128)(2,1)}) %reduce-scatter.16.cloned.1.call-update) | async-done | bytes 65552 | tf_op jit(solution)/shard_map/reduce_scatter | solution.py:251
  784.5 169.8 %all-reduce.20.cloned.1.call-done = bf16[3,1024,512]{2,0,1:T(4,128)(2,1)} async-done(((bf16[3,1024,512]{2,0,1:T(4,128)(2,1)}), bf16[3,1024,512]{2,0,1:T(4,128)(2,1)}) %all-reduce.20.cloned.1.call-update) | async-done | bytes 3145744
  956.2 9.0 reduce-scatter.14.cloned.1.call-done
  966.9 1.9 fusion.35
  970.2 77.0 %all-reduce.16 = (bf16[1024]{0:T(1024)(128)(2,1)S(1)}, bf16[1024]{0:T(1024)(128)(2,1)S(1)}, bf16[1024]{0:T(1024)(128)(2,1)S(1)}, bf16[1024]{0:T(1024)(128)(2,1)S...) all-reduce(bf16[1024]{0:T(1024)(128)(2,1)S(1)} %dynamic-update-slic, ...), channel_id=1, replica_groups=mesh['dp'=16,'tensor'=2] {'dp'}, use_global_device_ids=true, to_apply=%add.6 | all-reduce | flops 9216 | bytes 36864
  1047.5 3.0 all-reduce.15
  1051.1 4.6 add_convert_fusion.1
  (187 shorter events, 43.6 us)
Async XLA Ops:
  7.2 89.3 %copy-start = (bf16[552,1024]{1,0:T(8,128)(2,1)S(1)}, bf16[552,1024]{1,0:T(8,128)(2,1)}, u32[]{:S(2)}) copy-start(bf16[552,1024]{1,0:T(8,128)(2,1)} %param.15) | copy-start | bytes 3391492
  7.2 97.6 %all-gather.9.cloned.1.call-start = ((), (), s32[]{:S(2)}) async-start(), calls=%async_computation.8 | async-start | bytes 3391488 | tf_op jit(solution)/shard_map/all_gather | solution.py:140
  92.0 3.8 copy-start.24
  93.5 6.0 copy-start.44
  93.5 6.6 copy-start.35
  98.0 78.4 %all-gather.11.cloned.1.call-start = ((), (), s32[]{:S(2)}) async-start(), calls=%async_computation.9 | async-start | bytes 3342336 | tf_op jit(solution)/shard_map/all_gather | solution.py:121
  98.7 139.1 %all-gather.13.cloned.1.call-start = ((), (), s32[]{:S(2)}) async-start(), calls=%async_computation.10 | async-start | bytes 1114112 | tf_op jit(solution)/shard_map/all_gather | solution.py:122
  99.4 152.0 %reduce-scatter.8.cloned.1.call-start = ((), (), s32[]{:S(2)}) async-start(), calls=%async_computation.11 | async-start | bytes 3391488 | tf_op jit(solution)/shard_map/reduce_scatter | solution.py:155
  185.0 5.0 copy-start.8
  187.1 18.6 %copy-start.6 = (bf16[1,1104,512]{1,2,0:T(8,128)(2,1)}, bf16[1,1104,512]{1,2,0:T(8,128)(2,1)S(1)}, u32[]{:S(2)}) copy-start(bf16[1,1104,512]{1,2,0:T(8,128)(2,1)S(1)} %copy.57) | copy-start | bytes 3391492
  205.7 16.2 %copy-start.13 = (bf16[1,1104,512]{1,2,0:T(8,128)(2,1)S(1)}, bf16[1,1104,512]{1,2,0:T(8,128)(2,1)}, u32[]{:S(2)}) copy-start(bf16[1,1104,512]{1,2,0:T(8,128)(2,1)} %copy.56) | copy-start | bytes 3391492
  237.7 4.5 copy-start.43
  242.3 89.0 %all-gather.17.cloned.1.call-start = ((), (), s32[]{:S(2)}) async-start(), calls=%async_computation.13 | async-start | bytes 4456448 | tf_op jit(solution)/shard_map/all_gather | solution.py:126
  242.9 99.9 %all-gather.15.cloned.1.call-start = ((), (), s32[]{:S(2)}) async-start(), calls=%async_computation.12 | async-start | bytes 3391488 | tf_op jit(solution)/shard_map/all_gather | solution.py:166
  244.1 242.1 %copy-start.20 = (f32[1024]{0:T(1024)}, f32[1024]{0:T(1024)S(1)}, u32[]{:S(2)}) copy-start(f32[1024]{0:T(1024)S(1)} %convert_element_type.213) | copy-start | bytes 12292
  244.2 243.3 %copy-start.18 = (f32[552]{0:T(1024)}, f32[552]{0:T(1024)S(1)}, u32[]{:S(2)}) copy-start(f32[552]{0:T(1024)S(1)} %fusion.40) | copy-start | bytes 6628
  255.9 2.8 copy-start.37
  255.9 101.0 %all-gather.21.cloned.1.call-start = ((), (), s32[]{:S(2)}) async-start(), calls=%async_computation.16 | async-start | bytes 3391488 | tf_op jit(solution)/shard_map/all_gather | solution.py:181
  257.9 179.0 %all-gather.19.cloned.1.call-start = ((), (), s32[]{:S(2)}) async-start(), calls=%async_computation.14 | async-start | bytes 4456448 | tf_op jit(solution)/shard_map/all_gather | solution.py:130
  258.7 224.3 %reduce-scatter.12.cloned.1.call-start = ((), (), s32[]{:S(2)}) async-start(), calls=%async_computation.17 | async-start | bytes 3391488 | tf_op jit(solution)/shard_map/reduce_scatter | solution.py:192
  436.9 31.2 %copy-start.38 = (bf16[1024,2048]{1,0:T(8,128)(2,1)S(1)}, bf16[1024,2048]{1,0:T(8,128)(2,1)}, u32[]{:S(2)}) copy-start(bf16[1024,2048]{1,0:T(8,128)(2,1)} %all-gather.17.cloned.1.call-done) | copy-start | bytes 12582916
  474.4 47.2 %all-gather.23.cloned.1.call-start = ((), (), s32[]{:S(2)}) async-start(), calls=%async_computation.18 | async-start | bytes 3391488 | tf_op jit(solution)/shard_map/all_gather | solution.py:203
  482.9 3.3 copy-start.11
  487.5 2.3 copy-start.4
  489.9 183.9 %reduce-scatter.20.cloned.1.call-start = ((), (), s32[]{:S(2)}) async-start(), calls=%async_computation.22 | async-start | bytes 4456448 | tf_op jit(solution)/shard_map/reduce_scatter | solution.py:269
  489.9 10.7 %copy-start.40 = (bf16[1104,1024]{1,0:T(8,128)(2,1)S(1)}, bf16[1104,1024]{1,0:T(8,128)(2,1)}, u32[]{:S(2)}) copy-start(bf16[1104,1024]{1,0:T(8,128)(2,1)} %all-gather.21.cloned.1.call-done) | copy-start | bytes 6782980
  510.2 193.3 %reduce-scatter.18.cloned.1.call-start = ((), (), s32[]{:S(2)}) async-start(), calls=%async_computation.21 | async-start | bytes 4456448 | tf_op jit(solution)/shard_map/reduce_scatter | solution.py:263
  521.3 261.7 %reduce-scatter.16.cloned.1.call-start = ((), (), s32[]{:S(2)}) async-start(), calls=%async_computation.20 | async-start | bytes 1114112 | tf_op jit(solution)/shard_map/reduce_scatter | solution.py:251
  526.2 16.6 %copy-start.14 = (bf16[1,1104,512]{1,2,0:T(8,128)(2,1)S(1)}, bf16[1,1104,512]{1,2,0:T(8,128)(2,1)}, u32[]{:S(2)}) copy-start(bf16[1,1104,512]{1,2,0:T(8,128)(2,1)} %copy.56) | copy-start | bytes 3391492
  575.1 33.6 %copy-start.9 = (bf16[1,1104,512]{1,2,0:T(8,128)(2,1)S(1)}, bf16[1,1104,512]{1,2,0:T(8,128)(2,1)}, u32[]{:S(2)}) copy-start(bf16[1,1104,512]{1,2,0:T(8,128)(2,1)} %copy-done.8) | copy-start | bytes 3391492
  620.5 5.1 copy-start.7
  625.2 329.2 %all-reduce.20.cloned.1.call-start = ((), (), s32[]{:S(2)}) async-start(), calls=%async_computation.23 | async-start | bytes 8388608
  653.6 311.6 %reduce-scatter.14.cloned.1.call-start = ((), (), s32[]{:S(2)}) async-start(), calls=%async_computation.19 | async-start | bytes 3391488 | tf_op jit(solution)/shard_map/reduce_scatter | solution.py:224
  661.7 389.3 %reduce-scatter.10.cloned.1.call-start = ((), (), s32[]{:S(2)}) async-start(), calls=%async_computation.15 | async-start | bytes 3391488 | tf_op jit(solution)/shard_map/reduce_scatter | solution.py:170
  673.7 293.1 %copy-start.1 = (bf16[552,1024]{1,0:T(8,128)(2,1)S(1)}, bf16[552,1024]{1,0:T(8,128)(2,1)}, u32[]{:S(2)}) copy-start(bf16[552,1024]{1,0:T(8,128)(2,1)} %param.15) | copy-start | bytes 3391492
  673.7 293.1 %copy-start.23 = (f32[552]{0:T(1024)S(1)}, f32[552]{0:T(1024)}, u32[]{:S(2)}) copy-start(f32[552]{0:T(1024)} %copy-done.22) | copy-start | bytes 6628
  673.7 293.1 %copy-start.25 = (f32[1024]{0:T(1024)S(1)}, f32[1024]{0:T(1024)}, u32[]{:S(2)}) copy-start(f32[1024]{0:T(1024)} %copy-done.24) | copy-start | bytes 12292
  955.4 13.5 %copy-start.29 = (f32[552]{0:T(1024)S(1)}, f32[552]{0:T(1024)}, u32[]{:S(2)}) copy-start(f32[552]{0:T(1024)} %copy-done.28) | copy-start | bytes 6628
  955.4 13.5 %copy-start.27 = (f32[552]{0:T(1024)S(1)}, f32[552]{0:T(1024)}, u32[]{:S(2)}) copy-start(f32[552]{0:T(1024)} %copy-done.26) | copy-start | bytes 6628
  965.3 3.6 copy-start.5
  966.8 3.4 copy-start.32
  966.9 3.4 copy-start.33
  966.9 3.4 copy-start.34
  966.9 3.4 copy-start.36
  966.9 84.1 %copy-start.3 = (bf16[552,1024]{1,0:T(8,128)(2,1)S(1)}, bf16[552,1024]{1,0:T(8,128)(2,1)}, u32[]{:S(2)}) copy-start(bf16[552,1024]{1,0:T(8,128)(2,1)} %reduce-scatter.8.cloned.1.call-done) | copy-start | bytes 3391492
  966.9 84.1 %copy-start.19 = (f32[552]{0:T(1024)S(1)}, f32[552]{0:T(1024)}, u32[]{:S(2)}) copy-start(f32[552]{0:T(1024)} %copy-done.18) | copy-start | bytes 6628
  966.9 84.1 %copy-start.21 = (f32[1024]{0:T(1024)S(1)}, f32[1024]{0:T(1024)}, u32[]{:S(2)}) copy-start(f32[1024]{0:T(1024)} %copy-done.20) | copy-start | bytes 12292
  966.9 84.1 %copy-start.31 = (f32[552]{0:T(1024)S(1)}, f32[552]{0:T(1024)}, u32[]{:S(2)}) copy-start(f32[552]{0:T(1024)} %copy-done.30) | copy-start | bytes 6628
  (14 other events, 22.4 us)
Sparse Core Ops, SparseCore 0:
  98.1 6.6 all-gather.8
  107.6 68.7 all-gather.10
  179.1 54.3 all-gather.12
  242.4 8.9 reduce-scatter.7
  254.0 77.2 all-gather.16
  333.3 9.4 all-gather.14
  344.9 11.9 all-gather.20
  359.7 77.2 all-gather.18
  474.5 8.3 reduce-scatter.11
  490.0 11.9 all-gather.22
  510.3 96.2 reduce-scatter.19
  608.7 94.7 reduce-scatter.17
  705.8 77.2 reduce-scatter.15
  789.5 164.8 all-reduce.19
  956.5 8.7 reduce-scatter.13
  967.4 10.9 reduce-scatter.9
